TPU v7x, 256 devices: a whole 4x4x8 slice. The times are simulated.
256 devices in a mesh: dp: 8 (over x, core), group: 32 (over z, y).
Axes of the slice: x: 4, y: 4, z: 8, core: 2. Of those that a mesh axis runs over, the one named last changes fastest.
Arguments:
- embeds: bfloat16 [65536, 1024], P(('dp', 'group')), may hold values from -6 to 6
- row_ids: int32 [65536], P(('dp', 'group')), may hold values from 0 to 63
- neighbors: int32 [256, 3], P('dp'), may hold values from 0 to 31, as said below
- w_first: bfloat16 [1024, 4096], P(None, 'dp'), may hold values from -0.1875 to 0.1875
- w_second: bfloat16 [4096, 1024], P('dp'), may hold values from -0.09375 to 0.09375
Outputs:
- grad_first: float32 [1024, 4096], P('group', 'dp')
- grad_second: float32 [4096, 1024], P('dp', 'group')
- grad_unit: float32 [65536, 1024], P(('dp', 'group'))
Inputs may be any that keep to these rules, and one draw needn't show every extreme that they name: `neighbors`: within a row the 3 entries differ from one another and from the row's own index b % 32.
All inputs are finite; a program needn't handle non-finite values.
Results may differ from a plain program's by a relative error of at most 0.013.
Values may be sent and summed in bfloat16 or wider, within the bound.
No kernel may reach another device: no remote copies, remote signals or barrier semaphores. Data moves between devices by JAX's collectives and lax.ppermute only.
A program may use at most 64 MiB of HBM per device.

v0:
```python
import jax
import jax.numpy as jnp
from jax import lax
from jax.sharding import PartitionSpec as P

EPS = 1e-06
TEMP = 10.0
SHIFT = -5.0


def gelu_fwd(value):
    return jax.nn.gelu(value, approximate=True)


def gelu_back(pre, grad):
    _, back = jax.vjp(gelu_fwd, pre)
    return back(grad)[0]


def per_device(embeds, row_ids, neighbors, w_first, w_second):
    owners = lax.axis_size("group")
    block = embeds.shape[0]
    piece = block // owners
    width = w_second.shape[1]
    listed = neighbors.shape[1]
    gathered = lax.all_gather(embeds, "dp", axis=0, tiled=True)
    pre = jnp.dot(gathered, w_first, preferred_element_type=jnp.float32)
    hidden = gelu_fwd(pre).astype(jnp.bfloat16)
    proj = lax.psum_scatter(
        jnp.dot(hidden, w_second, preferred_element_type=jnp.float32).astype(jnp.bfloat16),
        "dp",
        scatter_dimension=0,
        tiled=True,
    ).astype(jnp.float32)
    inv = lax.rsqrt(jnp.mean(proj * proj, axis=-1, keepdims=True) + EPS)
    unit = proj * inv
    unit_b = unit.astype(jnp.bfloat16)
    held, held_ids = (
        lax.all_to_all(
            unit_b.reshape(owners, piece, width), "group", split_axis=0, concat_axis=0, tiled=True
        ),
        lax.all_to_all(
            row_ids.reshape(owners, piece), "group", split_axis=0, concat_axis=0, tiled=True
        ),
    )
    order = neighbors.T
    outgoing = jnp.take(held, order, axis=0)
    outgoing_ids = jnp.take(held_ids, order, axis=0)
    fetched, fetched_ids = (
        lax.all_to_all(outgoing, "group", split_axis=1, concat_axis=1, tiled=True),
        lax.all_to_all(outgoing_ids, "group", split_axis=1, concat_axis=1, tiled=True),
    )
    cand = jnp.concatenate([unit_b[None], fetched.reshape(listed, block, width)], 0)
    cand_ids = jnp.concatenate([row_ids[None], fetched_ids.reshape(listed, block)], 0)
    logits = (
        TEMP / width * jnp.einsum("rp,kcp->krc", unit_b, cand, preferred_element_type=jnp.float32)
        + SHIFT
    )
    sign = jnp.where(row_ids[None, :, None] == cand_ids[:, None, :], 1.0, -1.0).astype(jnp.float32)
    weight = (-sign * jax.nn.sigmoid(-sign * logits) * (TEMP / width)).astype(jnp.bfloat16)
    grad_own = jnp.einsum("krc,kcp->rp", weight, cand, preferred_element_type=jnp.float32)
    grad_cand = jnp.einsum("krc,rp->kcp", weight, unit_b, preferred_element_type=jnp.float32)
    returned = lax.all_to_all(
        grad_cand[1:].reshape(listed, owners, piece, width),
        "group",
        split_axis=1,
        concat_axis=1,
        tiled=True,
    )
    select = (order[:, :, None] == jnp.arange(owners, dtype=jnp.int32)[None, None, :]).astype(
        jnp.float32
    )
    summed = jnp.einsum("krb,krqp->bqp", select, returned, precision=lax.Precision.HIGHEST)
    collected = lax.all_to_all(summed, "group", split_axis=0, concat_axis=0, tiled=True)
    grad_unit = grad_own + grad_cand[0] + collected.reshape(block, width)
    grad_proj = inv * (grad_unit - unit * jnp.mean(unit * grad_unit, axis=-1, keepdims=True))
    grad_all = lax.all_gather(grad_proj.astype(jnp.bfloat16), "dp", axis=0, tiled=True)
    second_local = lax.dot_general(
        hidden, grad_all, (((0,), (0,)), ((), ())), preferred_element_type=jnp.float32
    )
    grad_hidden = lax.dot_general(
        grad_all, w_second, (((1,), (1,)), ((), ())), preferred_element_type=jnp.float32
    )
    grad_pre = gelu_back(pre, grad_hidden).astype(jnp.bfloat16)
    first_local = lax.dot_general(
        gathered, grad_pre, (((0,), (0,)), ((), ())), preferred_element_type=jnp.float32
    )
    first_out, second_out = (
        lax.psum_scatter(first_local, "group", scatter_dimension=0, tiled=True),
        lax.psum_scatter(second_local, "group", scatter_dimension=1, tiled=True),
    )
    return (first_out, second_out, grad_unit)


def solution(mesh):
    in_specs = (
        P(("dp", "group"), None),
        P(("dp", "group")),
        P("dp", None),
        P(None, "dp"),
        P("dp", None),
    )
    out_specs = (P("group", "dp"), P("dp", "group"), P(("dp", "group"), None))
    return jax.shard_map(
        per_device, mesh=mesh, in_specs=in_specs, out_specs=out_specs, check_vma=False
    )
```

profile of v0, /device:TPU:4, one launch (start us, length us, event | category | flops | bytes accessed | tf_op | source)
XLA Modules:
  0.0 792.0 jit_solution(12244141082356973376)
XLA Ops:
  8.0 38.2 %all-gather.3.cloned.1.call-done = bf16[2048,1024]{1,0:T(8,128)(2,1)} async-done(((bf16[256,1024]{1,0:T(8,128)(2,1)}), bf16[2048,1024]{1,0:T(8,128)(2,1)}) %all-gather.3.cloned.1.call-update) | async-done | bytes 4194320 | tf_op jit(solution)/shard_map/all_gather | solution.py:26
  46.2 4.8 fusion.58
  51.0 2.0 copy-done.6
  53.0 4.8 convolution_convert_fusion
  59.1 9.9 %all-to-all-start = ((s32[32,1,8]{2,1,0:T(1,128)}), s32[32,1,8]{2,1,0:T(1,128)S(1)}, u32[]{:S(2)}, u32[]{:S(2)}) async-start(s32[32,1,8]{2,1,0:T(1,128)} %bitcast.2), calls=%async_computation.1 | async-start | bytes 32768 | tf_op jit(solution)/shard_map/all_to_all | solution.py:42
  69.0 26.2 %reduce-scatter.6.cloned.1.call-done = bf16[256,1024]{1,0:T(8,128)(2,1)} async-done(((bf16[2048,1024]{1,0:T(8,128)(2,1)}), bf16[256,1024]{1,0:T(8,128)(2,1)}) %reduce-scatter.6.cloned.1.call-update) | async-done | bytes 524304 | tf_op jit(solution)/shard_map/reduce_scatter | solution.py:29
  96.4 2.2 fusion.54
  98.6 9.6 %all-to-all-start.2 = ((bf16[32,8,1024]{2,1,0:T(8,128)(2,1)}), bf16[32,8,1024]{2,1,0:T(8,128)(2,1)S(1)}, u32[]{:S(2)}, u32[]{:S(2)}) async-start(bf16[32,8,1024]{2,1,0:T(8,128)(2,1)} %get-tuple-element.19), calls=%async_computation.3 | async-start | bytes 1048576 | tf_op jit(solution)/shard_map/all_to_all | solution.py:39
  109.8 16.9 %all-to-all-done.2 = bf16[32,8,1024]{2,1,0:T(8,128)(2,1)S(1)} async-done(((bf16[32,8,1024]{2,1,0:T(8,128)(2,1)}), bf16[32,8,1024]{2,1,0:T(8,128)(2,1)S(1)}, u32[]{:S(2)}, u32[]{:S(2)}) %all-to-all-start.2) | async-done | bytes 524320 | tf_op jit(solution)/shard_map/all_to_all | solution.py:39
  126.8 4.7 all-to-all-start.1
  132.4 1.3 copy.46
  133.8 7.7 all-to-all-done.1
  141.5 4.0 all-to-all-start.3
  145.6 37.7 %all-to-all-done.3 = bf16[3,32,8,1024]{3,2,0,1:T(8,128)(2,1)S(1)} async-done(((bf16[3,32,8,1024]{3,2,0,1:T(8,128)(2,1)}), bf16[3,32,8,1024]{3,2,0,1:T(8,128)(2,1)S(1)}, u32[]{:S(2)}, u32[]{:S(2)}) %all-to-all-start.3) | async-done | bytes 1572896 | tf_op jit(solution)/shard_map/all_to_all | solution.py:50
  183.5 2.1 fusion.31
  187.2 75.9 %all_to_all.37 = f32[3,32,8,1024]{3,2,0,1:T(8,128)S(1)} all-to-all(f32[3,32,8,1024]{3,2,0,1:T(8,128)S(1)} %copy.50), channel_id=1, replica_groups=mesh['dp'=8,'group'=32] {'group'}, dimensions={1} | all-to-all | bytes 6291456 | tf_op jit(solution)/shard_map/all_to_all | solution.py:63
  263.2 3.1 fusion.14
  266.9 31.0 %all_to_all.38 = f32[32,8,1024]{2,1,0:T(8,128)S(1)} all-to-all(f32[32,8,1024]{2,1,0:T(8,128)S(1)} %copy.52), channel_id=1, replica_groups=mesh['dp'=8,'group'=32] {'group'}, dimensions={0} | all-to-all | bytes 2097152 | tf_op jit(solution)/shard_map/all_to_all | solution.py:74
  300.9 33.7 %all-gather.5.cloned.1.call-done = bf16[2048,1024]{1,0:T(8,128)(2,1)} async-done(((bf16[256,1024]{1,0:T(8,128)(2,1)}), bf16[2048,1024]{1,0:T(8,128)(2,1)}) %all-gather.5.cloned.1.call-update) | async-done | bytes 4194320 | tf_op jit(solution)/shard_map/all_gather | solution.py:77
  334.6 11.6 %fusion.11 = f32[1024,512]{0,1:T(8,128)S(1)} fusion(bf16[2048,1024]{1,0:T(8,128)(2,1)} %all-gather.3.cloned.1.call-done, f32[2048,512]{1,0:T(8,128)} %copy-done.6, bf16[2048,1024]{1,0:T(8,128)(2,1)} %all-gather.5.cloned.1.call-done, bf16[512,1024]{1,0:T(8,128)(2,1)S(1)} %copy-done), kind=kOutput, calls=%fused_computation.18 | convolution fusion | flops 4315938816 | bytes 15728640 | tf_op jit(solution)/shard_map/dot_general | solution.py:85
  346.2 1.9 copy.56
  348.1 7.3 fusion.55
  355.5 210.5 %reduce-scatter.10.cloned.1.call-done = f32[32,512]{1,0:T(8,128)} async-done(((f32[1024,512]{1,0:T(8,128)}), f32[32,512]{1,0:T(8,128)}) %reduce-scatter.10.cloned.1.call-update) | async-done | bytes 65552
  566.0 219.4 %reduce-scatter.8.cloned.1.call-done = f32[512,32]{0,1:T(8,128)} async-done(((f32[512,1024]{0,1:T(8,128)}), f32[512,32]{0,1:T(8,128)}) %reduce-scatter.8.cloned.1.call-update) | async-done | bytes 65552 | tf_op jit(solution)/shard_map/reduce_scatter | solution.py:90
  (47 shorter events, 11.5 us)
Async XLA Ops:
  7.2 45.8 %copy-start = (bf16[512,1024]{1,0:T(8,128)(2,1)S(1)}, bf16[512,1024]{1,0:T(8,128)(2,1)}, u32[]{:S(2)}) copy-start(bf16[512,1024]{1,0:T(8,128)(2,1)} %param.9) | copy-start | bytes 3145732
  7.2 39.0 %all-gather.3.cloned.1.call-start = ((), (), s32[]{:S(2)}) async-start(), calls=%async_computation.9 | async-start | bytes 4718592 | tf_op jit(solution)/shard_map/all_gather | solution.py:26
  7.9 87.3 %reduce-scatter.6.cloned.1.call-start = ((), (), s32[]{:S(2)}) async-start(), calls=%async_computation.10 | async-start | bytes 4718592 | tf_op jit(solution)/shard_map/reduce_scatter | solution.py:29
  51.0 2.0 copy-start.6
  57.8 0.7 copy-start.5
  57.8 50.5 %copy-start.4 = (s32[32,3]{0,1:T(4,128)S(1)}, s32[32,3]{0,1:T(4,128)}, u32[]{:S(2)}) copy-start(s32[32,3]{0,1:T(4,128)} %param.7) | copy-start | bytes 1156
  59.1 39.5 %all-to-all-start = ((s32[32,1,8]{2,1,0:T(1,128)}), s32[32,1,8]{2,1,0:T(1,128)S(1)}, u32[]{:S(2)}, u32[]{:S(2)}) async-start(s32[32,1,8]{2,1,0:T(1,128)} %bitcast.2), calls=%async_computation.1 | async-start | bytes 32768 | tf_op jit(solution)/shard_map/all_to_all | solution.py:42
  98.6 28.1 %all-to-all-start.2 = ((bf16[32,8,1024]{2,1,0:T(8,128)(2,1)}), bf16[32,8,1024]{2,1,0:T(8,128)(2,1)S(1)}, u32[]{:S(2)}, u32[]{:S(2)}) async-start(bf16[32,8,1024]{2,1,0:T(8,128)(2,1)} %get-tuple-element.19), calls=%async_computation.3 | async-start | bytes 1048576 | tf_op jit(solution)/shard_map/all_to_all | solution.py:39
  126.8 14.7 %all-to-all-start.1 = ((s32[3,32,8]{2,0,1:T(4,128)}), s32[3,32,8]{2,0,1:T(4,128)S(1)}, u32[]{:S(2)}, u32[]{:S(2)}) async-start(s32[3,32,8]{2,0,1:T(4,128)} %copy_select_fusion), calls=%async_computation.2 | async-start | bytes 131072 | tf_op jit(solution)/shard_map/all_to_all | solution.py:51
  132.4 51.0 %copy-start.1 = (bf16[256,1024]{1,0:T(8,128)(2,1)S(1)}, bf16[256,1024]{1,0:T(8,128)(2,1)}, u32[]{:S(2)}) copy-start(bf16[256,1024]{1,0:T(8,128)(2,1)} %reduce-scatter.6.cloned.1.call-done) | copy-start | bytes 1572868
  141.5 41.9 %all-to-all-start.3 = ((bf16[3,32,8,1024]{3,2,0,1:T(8,128)(2,1)}), bf16[3,32,8,1024]{3,2,0,1:T(8,128)(2,1)S(1)}, u32[]{:S(2)}, u32[]{:S(2)}) async-start(bf16[3,32,8,1024]{3,2,0,1:T(8,128)(2,1)} %copy.46), calls=%async_computation.4 | async-start | bytes 3145728 | tf_op jit(solution)/shard_map/all_to_all | solution.py:50
  145.5 189.2 %all-gather.5.cloned.1.call-start = ((), (), s32[]{:S(2)}) async-start(), calls=%async_computation.11 | async-start | bytes 4718592 | tf_op jit(solution)/shard_map/all_gather | solution.py:77
  263.2 34.7 %copy-start.3 = (bf16[1,256,1024]{2,1,0:T(8,128)(2,1)S(1)}, bf16[1,256,1024]{2,1,0:T(8,128)(2,1)}, u32[]{:S(2)}) copy-start(bf16[1,256,1024]{2,1,0:T(8,128)(2,1)} %get-tuple-element.18) | copy-start | bytes 1572868
  298.8 1.0 copy-start.2
  300.9 265.1 %reduce-scatter.10.cloned.1.call-start = ((), (), s32[]{:S(2)}) async-start(), calls=%async_computation.13 | async-start | bytes 2162688
  348.1 437.3 %reduce-scatter.8.cloned.1.call-start = ((), (), s32[]{:S(2)}) async-start(), calls=%async_computation.12 | async-start | bytes 2162688 | tf_op jit(solution)/shard_map/reduce_scatter | solution.py:90
Sparse Core Ops, SparseCore 0:
  9.9 36.2 all-gather.2
  57.9 37.2 reduce-scatter.5
  301.0 33.5 all-gather.4
  348.2 217.7 reduce-scatter.9
  570.7 214.6 reduce-scatter.7
where the time goes:
time: 793 us; the launch traced here: 792 us
  waiting for transfers between devices  591 us (75%)
  blocking collectives  107 us (13%)
  matrix products  35.4 us (4%)
  starting transfers between devices  28.3 us (4%)
  between operations  14 us (2%)
  local copies, waits for them, and re-layouts  10.6 us (1%)
    reduce_scatter x1, waiting for transfers between devices, per_device(): lax.psum_scatter(second_local, 'group', scatter_dimension=1, tiled=True)  219 us
    unnamed x6, waiting for transfers between devices  211 us
    all_to_all x1, blocking collectives, per_device(): lax.all_to_all(grad_cand[1:].reshape(listed, owners, piece, width), 'grou...  75.9 us
    all_gather x1, waiting for transfers between devices, per_device(): gathered = lax.all_gather(embeds, 'dp', axis=0, tiled=True)  38.2 us
    all_to_all x1, waiting for transfers between devices, per_device(): lax.all_to_all(outgoing, 'group', split_axis=1, concat_axis=1, tiled=True)  37.7 us
    all_gather x1, waiting for transfers between devices, per_device(): lax.all_gather(grad_proj.astype(jnp.bfloat16), 'dp', axis=0, tiled=True)  33.7 us
    all_to_all x1, blocking collectives, per_device(): lax.all_to_all(summed, 'group', split_axis=0, concat_axis=0, tiled=True)  31 us
    reduce_scatter x1, waiting for transfers between devices, per_device(): lax.psum_scatter(jnp.dot(hidden, w_second, preferred_element_type=jnp.flo...  26.2 us
  transfers between devices with their start and end apart: 9, of which 8 were waited for; matrix products, arithmetic and copies ran while one was open for 2% of the time, Pallas kernels for 0%

commit v1 on v0

--- a/solution.py
+++ b/solution.py
@@ -2,6 +2,7 @@
 import jax.numpy as jnp
 from jax import lax
 from jax.sharding import PartitionSpec as P
+from jax.lax import axis_index, axis_size, ppermute
 
 EPS = 1e-06
 TEMP = 10.0
@@ -23,7 +24,25 @@
     piece = block // owners
     width = w_second.shape[1]
     listed = neighbors.shape[1]
-    gathered = lax.all_gather(embeds, "dp", axis=0, tiled=True)
+    s_next = axis_index("dp")
+    newest = axis_size("dp")
+    everything, found_now, opened = (newest, s_next, embeds.shape[0])
+    pieces_in = [(it, (it + 1) % everything) for it in range(everything)]
+    column = [(it, (it - 1) % everything) for it in range(everything)]
+    gathered = jnp.zeros((*embeds.shape[:0], everything * opened, *embeds.shape[1:]), embeds.dtype)
+    gathered = lax.dynamic_update_slice_in_dim(gathered, embeds, found_now * opened, axis=0)
+    b_now = everything // 2
+    p_next = a_next = embeds
+    for nth in range(1, b_now + 1):
+        p_next = ppermute(p_next, "dp", pieces_in)
+        gathered = lax.dynamic_update_slice_in_dim(
+            gathered, p_next, (found_now - nth) % everything * opened, axis=0
+        )
+        if nth < everything - b_now:
+            a_next = ppermute(a_next, "dp", perm=column)
+            gathered = lax.dynamic_update_slice_in_dim(
+                gathered, a_next, (found_now + nth) % everything * opened, axis=0
+            )
     pre = jnp.dot(gathered, w_first, preferred_element_type=jnp.float32)
     hidden = gelu_fwd(pre).astype(jnp.bfloat16)
     proj = lax.psum_scatter(

time: 793 us -> 785 us (0.990)
  waiting for transfers between devices: 591 us -> 577 us
    reduce_scatter x0 -> x1, waiting for transfers between devices: none -> 219 us  [per_device(): lax.psum_scatter(first_local, 'group', scatter_dimension=0, tiled=True)]
    unnamed x6 -> x4, waiting for transfers between devices: 211 us -> 0.07 us
    all_gather x1 -> x0, waiting for transfers between devices: 38.2 us -> none  [per_device(): gathered = lax.all_gather(embeds, 'dp', axis=0, tiled=True)]
    ppermute x0 -> x7, waiting for transfers between devices: none -> 27.7 us  [the longest x4 27.7 us: per_device(): p_next = ppermute(p_next, 'dp', pieces_in)]
    reduce_scatter x1, waiting for transfers between devices: 219 us -> 205 us  [per_device(): lax.psum_scatter(second_local, 'group', scatter_dimension=1, tiled=True)]
  transfers between devices with their start and end apart: 9 -> 15, of which waited for: 8 -> 11; matrix products, arithmetic and copies ran while one was open for 2% -> 3% of each run, Pallas kernels for 0% -> 0%
where the time goes in v1:
time: 785 us; the launch traced here: 784 us
  waiting for transfers between devices  577 us (74%)
  blocking collectives  107 us (14%)
  starting transfers between devices  35.7 us (5%)
  matrix products  33.5 us (4%)
  between operations  14.1 us (2%)
  local copies, waits for them, and re-layouts  11.7 us (1%)
    reduce_scatter x1, waiting for transfers between devices, per_device(): lax.psum_scatter(first_local, 'group', scatter_dimension=0, tiled=True)  219 us
    reduce_scatter x1, waiting for transfers between devices, per_device(): lax.psum_scatter(second_local, 'group', scatter_dimension=1, tiled=True)  205 us
    all_to_all x1, blocking collectives, per_device(): lax.all_to_all(grad_cand[1:].reshape(listed, owners, piece, width), 'grou...  75.9 us
    all_to_all x1, waiting for transfers between devices, per_device(): lax.all_to_all(outgoing, 'group', split_axis=1, concat_axis=1, tiled=True)  37.7 us
    all_gather x1, waiting for transfers between devices, per_device(): lax.all_gather(grad_proj.astype(jnp.bfloat16), 'dp', axis=0, tiled=True)  33.6 us
    all_to_all x1, blocking collectives, per_device(): lax.all_to_all(summed, 'group', split_axis=0, concat_axis=0, tiled=True)  31 us
    reduce_scatter x1, waiting for transfers between devices, per_device(): lax.psum_scatter(jnp.dot(hidden, w_second, preferred_element_type=jnp.flo...  28.4 us
    ppermute x4, waiting for transfers between devices, per_device(): p_next = ppermute(p_next, 'dp', pieces_in)  27.7 us
  transfers between devices with their start and end apart: 15, of which 11 were waited for; matrix products, arithmetic and copies ran while one was open for 3% of the time, Pallas kernels for 0%

profile of v1, /device:TPU:4, one launch (start us, length us, event | category | flops | bytes accessed | tf_op | source)
XLA Modules:
  0.0 784.4 jit_solution(5708823436211058588)
XLA Ops:
  9.0 7.1 collective-permute-done
  17.8 7.0 collective-permute-done.2
  27.2 6.4 collective-permute-done.4
  34.9 7.3 collective-permute-done.6
  44.2 2.3 fusion.55
  48.6 4.7 convolution_convert_fusion
  54.7 11.5 %all-to-all-start = ((s32[32,1,8]{2,1,0:T(1,128)}), s32[32,1,8]{2,1,0:T(1,128)S(1)}, u32[]{:S(2)}, u32[]{:S(2)}) async-start(s32[32,1,8]{2,1,0:T(1,128)} %bitcast.2), calls=%async_computation.1 | async-start | bytes 32768 | tf_op jit(solution)/shard_map/all_to_all | solution.py:61
  66.2 28.4 %reduce-scatter.4.cloned.1.call-done = bf16[256,1024]{1,0:T(8,128)(2,1)} async-done(((bf16[2048,1024]{1,0:T(8,128)(2,1)}), bf16[256,1024]{1,0:T(8,128)(2,1)}) %reduce-scatter.4.cloned.1.call-update) | async-done | bytes 524304 | tf_op jit(solution)/shard_map/reduce_scatter | solution.py:48
  95.8 2.2 fusion.51
  98.0 9.7 %all-to-all-start.2 = ((bf16[32,8,1024]{2,1,0:T(8,128)(2,1)}), bf16[32,8,1024]{2,1,0:T(8,128)(2,1)S(1)}, u32[]{:S(2)}, u32[]{:S(2)}) async-start(bf16[32,8,1024]{2,1,0:T(8,128)(2,1)} %get-tuple-element.4), calls=%async_computation.3 | async-start | bytes 1048576 | tf_op jit(solution)/shard_map/all_to_all | solution.py:58
  109.3 16.8 %all-to-all-done.2 = bf16[32,8,1024]{2,1,0:T(8,128)(2,1)S(1)} async-done(((bf16[32,8,1024]{2,1,0:T(8,128)(2,1)}), bf16[32,8,1024]{2,1,0:T(8,128)(2,1)S(1)}, u32[]{:S(2)}, u32[]{:S(2)}) %all-to-all-start.2) | async-done | bytes 524320 | tf_op jit(solution)/shard_map/all_to_all | solution.py:58
  126.2 4.9 all-to-all-start.1
  133.3 7.7 all-to-all-done.1
  141.0 4.0 all-to-all-start.3
  145.2 37.7 %all-to-all-done.3 = bf16[3,32,8,1024]{3,2,0,1:T(8,128)(2,1)S(1)} async-done(((bf16[3,32,8,1024]{3,2,0,1:T(8,128)(2,1)}), bf16[3,32,8,1024]{3,2,0,1:T(8,128)(2,1)S(1)}, u32[]{:S(2)}, u32[]{:S(2)}) %all-to-all-start.3) | async-done | bytes 1572896 | tf_op jit(solution)/shard_map/all_to_all | solution.py:69
  183.0 2.1 fusion.28
  186.8 75.9 %all_to_all.37 = f32[3,32,8,1024]{3,2,0,1:T(8,128)S(1)} all-to-all(f32[3,32,8,1024]{3,2,0,1:T(8,128)S(1)} %copy.46), channel_id=1, replica_groups=mesh['dp'=8,'group'=32] {'group'}, dimensions={1} | all-to-all | bytes 6291456 | tf_op jit(solution)/shard_map/all_to_all | solution.py:82
  262.7 3.1 fusion.11
  266.4 31.0 %all_to_all.38 = f32[32,8,1024]{2,1,0:T(8,128)S(1)} all-to-all(f32[32,8,1024]{2,1,0:T(8,128)S(1)} %copy.48), channel_id=1, replica_groups=mesh['dp'=8,'group'=32] {'group'}, dimensions={0} | all-to-all | bytes 2097152 | tf_op jit(solution)/shard_map/all_to_all | solution.py:93
  299.6 33.6 %all-gather.2.cloned.1.call-done = bf16[2048,1024]{1,0:T(8,128)(2,1)} async-done(((bf16[256,1024]{1,0:T(8,128)(2,1)}), bf16[2048,1024]{1,0:T(8,128)(2,1)}) %all-gather.2.cloned.1.call-update) | async-done | bytes 4194320 | tf_op jit(solution)/shard_map/all_gather | solution.py:96
  333.3 7.3 fusion.52
  340.8 12.2 %fusion.9 = f32[1024,512]{1,0:T(8,128)} fusion(bf16[2048,1024]{1,0:T(8,128)(2,1)} %copy-done.2, f32[2048,512]{1,0:T(8,128)} %copy-done.11, bf16[2048,1024]{1,0:T(8,128)(2,1)} %all-gather.2.cloned.1.call-done, bf16[512,1024]{1,0:T(8,128)(2,1)S(1)} %copy-done), kind=kOutput, calls=%fused_computation.17 | convolution fusion | flops 4315938816 | bytes 15728640 | tf_op jit(solution)/shard_map/dot_general | solution.py:104
  353.1 205.4 %reduce-scatter.8.cloned.1.call-done = f32[512,32]{0,1:T(8,128)} async-done(((f32[512,1024]{0,1:T(8,128)}), f32[512,32]{0,1:T(8,128)}) %reduce-scatter.8.cloned.1.call-update) | async-done | bytes 65552 | tf_op jit(solution)/shard_map/reduce_scatter | solution.py:109
  558.5 219.4 %reduce-scatter.6.cloned.1.call-done = f32[32,512]{1,0:T(8,128)} async-done(((f32[1024,512]{1,0:T(8,128)}), f32[32,512]{1,0:T(8,128)}) %reduce-scatter.6.cloned.1.call-update) | async-done | bytes 65552 | tf_op jit(solution)/shard_map/reduce_scatter | solution.py:108
  (76 shorter events, 22.6 us)
Async XLA Ops:
  7.2 41.4 %copy-start = (bf16[512,1024]{1,0:T(8,128)(2,1)S(1)}, bf16[512,1024]{1,0:T(8,128)(2,1)}, u32[]{:S(2)}) copy-start(bf16[512,1024]{1,0:T(8,128)(2,1)} %param.9) | copy-start | bytes 3145732
  7.2 18.1 %copy-start.4 = (bf16[256,1024]{1,0:T(8,128)(2,1)S(1)}, bf16[256,1024]{1,0:T(8,128)(2,1)}, u32[]{:S(2)}) copy-start(bf16[256,1024]{1,0:T(8,128)(2,1)} %param.5) | copy-start | bytes 1572868
  7.2 87.4 %reduce-scatter.4.cloned.1.call-start = ((), (), s32[]{:S(2)}) async-start(), calls=%async_computation.9 | async-start | bytes 4718592 | tf_op jit(solution)/shard_map/reduce_scatter | solution.py:48
  7.2 8.8 %collective-permute-start = (bf16[256,1024]{1,0:T(8,128)(2,1)}, bf16[256,1024]{1,0:T(8,128)(2,1)S(1)}, u32[]{:S(2)}, u32[]{:S(2)}) collective-permute-start(bf16[256,1024]{1,0:T(8,128)(2,1)} %param.5), channel_id=1, source_target_pairs={{0,32},{32,64},{64,96},{96,128},{128,160},{160,192},{192,224},{224... | collective-permute-start | bytes 1572872 | tf_op jit(solution)/shard_map/ppermute | solution.py:37
  7.3 8.8 %collective-permute-start.1 = (bf16[256,1024]{1,0:T(8,128)(2,1)}, bf16[256,1024]{1,0:T(8,128)(2,1)S(1)}, u32[]{:S(2)}, u32[]{:S(2)}) collective-permute-start(bf16[256,1024]{1,0:T(8,128)(2,1)} %param.5), channel_id=1, source_target_pairs={{0,224},{32,0},{64,32},{96,64},{128,96},{160,128},{192,160},{224,1... | collective-permute-start | bytes 1572872 | tf_op jit(solution)/shard_map/ppermute | solution.py:42
  16.1 8.7 %collective-permute-start.2 = (bf16[256,1024]{1,0:T(8,128)(2,1)S(1)}, bf16[256,1024]{1,0:T(8,128)(2,1)}, u32[]{:S(2)}, u32[]{:S(2)}) collective-permute-start(bf16[256,1024]{1,0:T(8,128)(2,1)S(1)} %collective-permute-done), channel_id=1, source_target_pairs={{0,32},{32,64},{64,96},{96,128},{128,160},{160,192},{192,224},{224... | collective-permute-start | bytes 1572872 | tf_op jit(solution)/shard_map/ppermute | solution.py:37
  16.1 9.3 %collective-permute-start.3 = (bf16[256,1024]{1,0:T(8,128)(2,1)S(1)}, bf16[256,1024]{1,0:T(8,128)(2,1)S(1)}, u32[]{:S(2)}, u32[]{:S(2)}) collective-permute-start(bf16[256,1024]{1,0:T(8,128)(2,1)S(1)} %collective-permute-done.1), channel_id=1, source_target_pairs={{0,224},{32,0},{64,32},{96,64},{128,96},{160,128},{192,160},{224,1... | collective-permute-start | bytes 1572872 | tf_op jit(solution)/shard_map/ppermute | solution.py:42
  24.8 8.8 %collective-permute-start.4 = (bf16[256,1024]{1,0:T(8,128)(2,1)}, bf16[256,1024]{1,0:T(8,128)(2,1)S(1)}, u32[]{:S(2)}, u32[]{:S(2)}) collective-permute-start(bf16[256,1024]{1,0:T(8,128)(2,1)} %collective-permute-done.2), channel_id=1, source_target_pairs={{0,32},{32,64},{64,96},{96,128},{128,160},{160,192},{192,224},{224... | collective-permute-start | bytes 1572872 | tf_op jit(solution)/shard_map/ppermute | solution.py:37
  24.8 2.4 copy-start.6
  25.3 18.9 %copy-start.10 = (bf16[1024,512]{1,0:T(8,128)(2,1)S(1)}, bf16[1024,512]{1,0:T(8,128)(2,1)}, u32[]{:S(2)}) copy-start(bf16[1024,512]{1,0:T(8,128)(2,1)} %param.8) | copy-start | bytes 3145732
  25.4 9.4 %collective-permute-start.5 = (bf16[256,1024]{1,0:T(8,128)(2,1)S(1)}, bf16[256,1024]{1,0:T(8,128)(2,1)S(1)}, u32[]{:S(2)}, u32[]{:S(2)}) collective-permute-start(bf16[256,1024]{1,0:T(8,128)(2,1)S(1)} %collective-permute-done.3), channel_id=1, source_target_pairs={{0,224},{32,0},{64,32},{96,64},{128,96},{160,128},{192,160},{224,1... | collective-permute-start | bytes 1572872 | tf_op jit(solution)/shard_map/ppermute | solution.py:42
  33.6 8.6 %collective-permute-start.6 = (bf16[256,1024]{1,0:T(8,128)(2,1)S(1)}, bf16[256,1024]{1,0:T(8,128)(2,1)S(1)}, u32[]{:S(2)}, u32[]{:S(2)}) collective-permute-start(bf16[256,1024]{1,0:T(8,128)(2,1)S(1)} %collective-permute-done.4), channel_id=1, source_target_pairs={{0,32},{32,64},{64,96},{96,128},{128,160},{160,192},{192,224},{224... | collective-permute-start | bytes 1572872 | tf_op jit(solution)/shard_map/ppermute | solution.py:37
  46.5 2.0 copy-start.11
  53.3 54.5 %copy-start.8 = (s32[32,3]{0,1:T(4,128)S(1)}, s32[32,3]{0,1:T(4,128)}, u32[]{:S(2)}) copy-start(s32[32,3]{0,1:T(4,128)} %param.7) | copy-start | bytes 1156
  54.7 43.3 %all-to-all-start = ((s32[32,1,8]{2,1,0:T(1,128)}), s32[32,1,8]{2,1,0:T(1,128)S(1)}, u32[]{:S(2)}, u32[]{:S(2)}) async-start(s32[32,1,8]{2,1,0:T(1,128)} %bitcast.2), calls=%async_computation.1 | async-start | bytes 32768 | tf_op jit(solution)/shard_map/all_to_all | solution.py:61
  98.0 28.2 %all-to-all-start.2 = ((bf16[32,8,1024]{2,1,0:T(8,128)(2,1)}), bf16[32,8,1024]{2,1,0:T(8,128)(2,1)S(1)}, u32[]{:S(2)}, u32[]{:S(2)}) async-start(bf16[32,8,1024]{2,1,0:T(8,128)(2,1)} %get-tuple-element.4), calls=%async_computation.3 | async-start | bytes 1048576 | tf_op jit(solution)/shard_map/all_to_all | solution.py:58
  126.2 14.9 %all-to-all-start.1 = ((s32[3,32,8]{2,0,1:T(4,128)}), s32[3,32,8]{2,0,1:T(4,128)S(1)}, u32[]{:S(2)}, u32[]{:S(2)}) async-start(s32[3,32,8]{2,0,1:T(4,128)} %copy_select_fusion), calls=%async_computation.2 | async-start | bytes 131072 | tf_op jit(solution)/shard_map/all_to_all | solution.py:70
  132.0 51.0 %copy-start.1 = (bf16[256,1024]{1,0:T(8,128)(2,1)S(1)}, bf16[256,1024]{1,0:T(8,128)(2,1)}, u32[]{:S(2)}) copy-start(bf16[256,1024]{1,0:T(8,128)(2,1)} %reduce-scatter.4.cloned.1.call-done) | copy-start | bytes 1572868
  141.0 41.9 %all-to-all-start.3 = ((bf16[3,32,8,1024]{3,2,0,1:T(8,128)(2,1)}), bf16[3,32,8,1024]{3,2,0,1:T(8,128)(2,1)S(1)}, u32[]{:S(2)}, u32[]{:S(2)}) async-start(bf16[3,32,8,1024]{3,2,0,1:T(8,128)(2,1)} %copy.42), calls=%async_computation.4 | async-start | bytes 3145728 | tf_op jit(solution)/shard_map/all_to_all | solution.py:69
  145.0 188.3 %all-gather.2.cloned.1.call-start = ((), (), s32[]{:S(2)}) async-start(), calls=%async_computation.10 | async-start | bytes 4718592 | tf_op jit(solution)/shard_map/all_gather | solution.py:96
  262.7 34.7 %copy-start.7 = (bf16[1,256,1024]{2,1,0:T(8,128)(2,1)S(1)}, bf16[1,256,1024]{2,1,0:T(8,128)(2,1)}, u32[]{:S(2)}) copy-start(bf16[1,256,1024]{2,1,0:T(8,128)(2,1)} %get-tuple-element.3) | copy-start | bytes 1572868
  298.4 42.2 %copy-start.3 = (f32[256,1024]{1,0:T(8,128)}, f32[256,1024]{1,0:T(8,128)S(1)}, u32[]{:S(2)}) copy-start(f32[256,1024]{1,0:T(8,128)S(1)} %get-tuple-element.6) | copy-start | bytes 3145732
  299.6 258.9 %reduce-scatter.8.cloned.1.call-start = ((), (), s32[]{:S(2)}) async-start(), calls=%async_computation.12 | async-start | bytes 2162688 | tf_op jit(solution)/shard_map/reduce_scatter | solution.py:109
  340.6 437.3 %reduce-scatter.6.cloned.1.call-start = ((), (), s32[]{:S(2)}) async-start(), calls=%async_computation.11 | async-start | bytes 2162688 | tf_op jit(solution)/shard_map/reduce_scatter | solution.py:108
  (3 other events, 4.4 us)
Sparse Core Ops, SparseCore 0:
  53.5 41.0 reduce-scatter.3
  299.7 33.5 all-gather.1
  340.7 217.7 reduce-scatter.7
  563.2 214.6 reduce-scatter.5
